TPU v7x, 32 devices: a whole 2x2x4 slice. The times are simulated.
32 devices in a mesh: dp: 4 (over y, x), wide: 8 (over z, core).
Axes of the slice: x: 2, y: 2, z: 4, core: 2. Of those that a mesh axis runs over, the one named last changes fastest.
Arguments:
- clips: bfloat16 [4, 8, 4, 128, 512], P('dp', 'wide'), may hold values from -8 to 8
- w_spatial: bfloat16 [4608, 512], P(None, 'dp'), may hold values from -0.09375 to 0.09375
- w_time: bfloat16 [1536, 512], replicated, may hold values from -0.15625 to 0.15625
- norm_gain: float32 [512], replicated, may hold values from 0.1 to 1.9
- norm_bias: float32 [512], replicated, may hold values from -0.6 to 0.6
- grad_out: bfloat16 [4, 8, 512, 512], P('dp', None, 'wide'), may hold values from -6 to 6
Outputs:
- grad_clips: bfloat16 [4, 8, 4, 128, 512], P('dp', 'wide')
- spatial_grad: float32 [4608, 512], P('dp', 'wide')
- time_grad: float32 [1536, 512], P('dp', 'wide')
All inputs are finite; a program needn't handle non-finite values.
Results may differ from a plain program's by a relative error of at most 0.009.
Values may be sent and summed in bfloat16 or wider, within the bound.
No kernel may reach another device: no remote copies, remote signals or barrier semaphores. Data moves between devices by JAX's collectives and lax.ppermute only.
A program may use at most 128 MiB of HBM per device.

v0:
```python
import jax
import jax.numpy as jnp
from jax import lax
from jax.sharding import PartitionSpec as P

G = 32
FRAMES = 8
EPSILON = 1e-06
CONTRACT_ROWS = (((0,), (0,)), ((), ()))
CONTRACT_COLS = (((1,), (1,)), ((), ()))


def pad_frames(frames):
    return jnp.pad(frames, ((0, 0), (1, 1), (1, 1), (0, 0)))


def spatial_forward(frames, weights):
    frame_total, row_count, col_count, chan_count = frames.shape
    padded = pad_frames(frames)
    accum_out = jnp.zeros((frame_total * row_count * col_count, weights.shape[1]), jnp.float32)
    for tap_index in range(9):
        row_off, col_off = (tap_index // 3, tap_index % 3)
        window = padded[:, row_off : row_off + row_count, col_off : col_off + col_count, :].reshape(
            -1, chan_count
        )
        tap_weight = weights[tap_index * chan_count : (tap_index + 1) * chan_count]
        accum_out = accum_out + jnp.dot(window, tap_weight, preferred_element_type=jnp.float32)
    return accum_out.reshape(frame_total, row_count, col_count, -1)


def spatial_backward(frames, grad_hidden, weights):
    frame_total, row_count, col_count, chan_count = frames.shape
    padded_in = pad_frames(frames)
    padded_grad = pad_frames(grad_hidden)
    grad_flat = grad_hidden.reshape(-1, chan_count)
    grad_input = jnp.zeros((frame_total * row_count * col_count, chan_count), jnp.float32)
    tap_grads = []
    for tap_index in range(9):
        row_off, col_off = (tap_index // 3, tap_index % 3)
        window = padded_in[
            :, row_off : row_off + row_count, col_off : col_off + col_count, :
        ].reshape(-1, chan_count)
        tap_grads.append(
            lax.dot_general(window, grad_flat, CONTRACT_ROWS, preferred_element_type=jnp.float32)
        )
        flipped = padded_grad[
            :, 2 - row_off : 2 - row_off + row_count, 2 - col_off : 2 - col_off + col_count, :
        ].reshape(-1, chan_count)
        tap_weight = weights[tap_index * chan_count : (tap_index + 1) * chan_count]
        grad_input = grad_input + lax.dot_general(
            flipped, tap_weight, CONTRACT_COLS, preferred_element_type=jnp.float32
        )
    return (grad_input.reshape(frames.shape), jnp.concatenate(tap_grads, axis=0))


def norm_forward(hidden, norm_gain, norm_bias):
    frame_total, row_count, col_count, chan_count = hidden.shape
    grouped = hidden.astype(jnp.float32).reshape(
        frame_total, row_count * col_count, G, chan_count // G
    )
    group_mean = jnp.mean(grouped, axis=(1, 3), keepdims=True)
    centered = grouped - group_mean
    variance = jnp.mean(centered * centered, axis=(1, 3), keepdims=True)
    inv_std = lax.rsqrt(variance + EPSILON)
    normed = centered * inv_std
    preact = normed.reshape(hidden.shape) * norm_gain + norm_bias
    return (preact, normed, inv_std)


def norm_backward(grad_act, preact, normed, inv_std, norm_gain):
    sigmoid_z = jax.nn.sigmoid(preact)
    grad_pre = grad_act.astype(jnp.float32) * sigmoid_z * (1.0 + preact * (1.0 - sigmoid_z))
    grad_normed = (grad_pre * norm_gain).reshape(normed.shape)
    mean_grad = jnp.mean(grad_normed, axis=(1, 3), keepdims=True)
    mean_proj = jnp.mean(grad_normed * normed, axis=(1, 3), keepdims=True)
    return ((grad_normed - mean_grad - normed * mean_proj) * inv_std).reshape(preact.shape)


def temporal_backward(tiles, grad_out, w_time):
    clip_count, frame_total, pix_count, chan_count = tiles.shape
    grad_act = jnp.zeros(tiles.shape, jnp.float32)
    tap_grads = []
    for tap_index in range(3):
        kept = frame_total - tap_index
        earlier = tiles[:, :kept].reshape(-1, chan_count)
        later = grad_out[:, tap_index:].reshape(-1, chan_count)
        tap_grads.append(
            lax.dot_general(earlier, later, CONTRACT_ROWS, preferred_element_type=jnp.float32)
        )
        tap_weight = w_time[tap_index * chan_count : (tap_index + 1) * chan_count]
        back_part = lax.dot_general(
            later, tap_weight, CONTRACT_COLS, preferred_element_type=jnp.float32
        )
        back_part = back_part.reshape(clip_count, kept, pix_count, chan_count)
        grad_act = grad_act + jnp.pad(back_part, ((0, 0), (0, tap_index), (0, 0), (0, 0)))
    return (jnp.concatenate(tap_grads, axis=0), grad_act)


def shards(clips, w_spatial, w_time, norm_gain, norm_bias, grad_out):
    group_count, frame_count, row_count, col_count, chan_count = clips.shape
    frames = clips.reshape(group_count * frame_count, row_count, col_count, chan_count)
    weights = lax.all_gather(w_spatial, "dp", axis=1, tiled=True)
    hidden = spatial_forward(frames, weights).astype(jnp.bfloat16)
    preact, normed, inv_std = norm_forward(hidden, norm_gain, norm_bias)
    act = (
        jax.nn.silu(preact)
        .astype(jnp.bfloat16)
        .reshape(group_count, frame_count, row_count * col_count, chan_count)
    )
    tiles = lax.all_to_all(act, "wide", split_axis=2, concat_axis=1, tiled=True)
    tile_shape = tiles.shape
    by_clip = tiles.reshape(-1, FRAMES, tile_shape[2], tile_shape[3])
    grad_clipwise = grad_out.reshape(by_clip.shape)
    time_raw, grad_act = temporal_backward(by_clip, grad_clipwise, w_time)
    grad_act = grad_act.astype(jnp.bfloat16).reshape(tile_shape)
    returned = lax.all_to_all(grad_act, "wide", split_axis=1, concat_axis=2, tiled=True)
    grad_hidden = norm_backward(
        returned.reshape(frames.shape), preact, normed, inv_std, norm_gain
    ).astype(jnp.bfloat16)
    grad_input, spatial_raw = spatial_backward(frames, grad_hidden, weights)
    position_total = (
        group_count
        * frame_count
        * row_count
        * col_count
        * lax.axis_size("wide")
        * lax.axis_size("dp")
    )
    grad_scale = float(position_total) ** (-0.5)
    partial_pair = (
        lax.psum_scatter(spatial_raw, "wide", scatter_dimension=1, tiled=True),
        lax.psum_scatter(time_raw, "wide", scatter_dimension=1, tiled=True),
    )
    spatial_sum, time_sum = (
        lax.psum_scatter(partial_pair[0], "dp", scatter_dimension=0, tiled=True),
        lax.psum_scatter(partial_pair[1], "dp", scatter_dimension=0, tiled=True),
    )
    grad_clips = grad_input.astype(jnp.bfloat16).reshape(clips.shape)
    return (grad_clips, spatial_sum * grad_scale, time_sum * grad_scale)


def solution(mesh):
    return jax.shard_map(
        shards,
        mesh=mesh,
        in_specs=(
            P("dp", "wide", None, None, None),
            P(None, "dp"),
            P(),
            P(),
            P(),
            P("dp", None, "wide", None),
        ),
        out_specs=(P("dp", "wide", None, None, None), P("dp", "wide"), P("dp", "wide")),
        check_vma=False,
    )
```

profile of v0, /device:TPU:0, one launch (start us, length us, event | category | flops | bytes accessed | tf_op | source)
XLA Modules:
  0.0 337.8 jit_solution(4861131859740784181)
XLA Ops:
  11.1 2.3 fusion.15
  13.4 6.4 %all-to-all-start = ((bf16[1,8,64,512]{3,2,0,1:T(8,128)(2,1)}), bf16[1,8,64,512]{3,2,0,1:T(8,128)(2,1)S(1)}, u32[]{:S(2)}, u32[]{:S(2)}) async-start(bf16[1,8,64,512]{3,2,0,1:T(8,128)(2,1)} %fusion.15), calls=%async_computation | async-start | bytes 1048576 | tf_op jit(solution)/shard_map/all_to_all | solution.py:116
  20.1 2.5 pad_slice_fusion
  22.6 2.1 copy.46
  24.7 2.0 copy.40
  26.7 2.1 copy.41
  28.8 2.0 copy.42
  30.8 2.0 copy.43
  32.9 2.0 copy.44
  36.9 32.4 %all-gather.2.cloned.1.call-done = bf16[4608,512]{1,0:T(8,128)(2,1)} async-done(((bf16[4608,128]{1,0:T(8,128)(2,1)}), bf16[4608,512]{1,0:T(8,128)(2,1)}) %all-gather.2.cloned.1.call-update) | async-done | bytes 4718608 | tf_op jit(solution)/shard_map/all_gather | solution.py:102
  82.4 5.6 %reduce.16 = bf16[512,512]{1,0:T(8,128)(2,1)} reduce(bf16[512,1,1,512]{3,2,1,0:T(2,128)(2,1)} %bitcast.222, bf16[]{:T(256)} %broadcast.543), dimensions={1,2}, to_apply=%bitcast.194.reduce_sub_computation | reduce | bytes 1048578
  88.0 2.2 reshape.596
  90.2 20.0 %all_to_all.21 = bf16[8,2,16384]{2,1,0:T(2,128)(2,1)} all-to-all(bf16[8,2,16384]{2,1,0:T(2,128)(2,1)} %reshape.596), channel_id=1, replica_groups=mesh['dp'=4,'wide'=8] {'wide'}, dimensions={0} | all-to-all | bytes 1048576 | tf_op jit(solution)/shard_map/all_to_all | solution.py:110
  110.2 3.5 %reshape.597 = bf16[512,1,1,512]{3,2,1,0:T(2,128)(2,1)} reshape(bf16[8,2,16384]{2,1,0:T(2,128)(2,1)} %all_to_all.21) | data formatting | bytes 1048576
  116.4 2.0 pad_maximum_fusion
  118.4 3.6 %copy.53 = f32[1536,512]{0,1:T(8,128)} copy(f32[1536,512]{1,0:T(8,128)} %pad_maximum_fusion) | data formatting | bytes 6291456
  136.8 9.7 %copy.51 = f32[4608,512]{0,1:T(8,128)} copy(f32[4608,512]{1,0:T(8,128)} %fusion) | data formatting | bytes 18874368
  146.6 13.9 %reduce-scatter.15.cloned.1.call-done = f32[64,1536]{1,0:T(8,128)} async-done(((f32[512,1536]{1,0:T(8,128)}), f32[64,1536]{1,0:T(8,128)}) %reduce-scatter.15.cloned.1.call-update) | async-done | bytes 393232
  160.5 2.2 copy.54
  163.4 1.9 pad_slice_fusion.8
  166.8 94.7 %reduce-scatter.13.cloned.1.call-done = f32[64,4608]{1,0:T(8,128)} async-done(((f32[512,4608]{1,0:T(8,128)}), f32[64,4608]{1,0:T(8,128)}) %reduce-scatter.13.cloned.1.call-update) | async-done | bytes 1179664
  261.5 2.9 copy.52
  273.1 15.9 %reduce-scatter.11.cloned.1.call-done = f32[384,64]{1,0:T(8,128)} async-done(((f32[1536,64]{1,0:T(8,128)}), f32[384,64]{1,0:T(8,128)}) %reduce-scatter.11.cloned.1.call-update) | async-done | bytes 98320 | tf_op jit(solution)/shard_map/reduce_scatter | solution.py:136
  290.6 38.6 %reduce-scatter.9.cloned.1.call-done = f32[1152,64]{1,0:T(8,128)} async-done(((f32[4608,64]{1,0:T(8,128)}), f32[1152,64]{1,0:T(8,128)}) %reduce-scatter.9.cloned.1.call-update) | async-done | bytes 294928 | tf_op jit(solution)/shard_map/reduce_scatter | solution.py:135
  (115 shorter events, 51.1 us)
Async XLA Ops:
  7.2 3.9 %copy-start.1 = (bf16[1,8,64,512]{3,2,1,0:T(8,128)(2,1)S(1)}, bf16[1,8,64,512]{3,2,1,0:T(8,128)(2,1)}, u32[]{:S(2)}) copy-start(bf16[1,8,64,512]{3,2,1,0:T(8,128)(2,1)} %param.11) | copy-start | bytes 1572868
  7.2 12.6 %copy-start.2 = (bf16[1,1,4,128,512]{4,3,2,1,0:T(8,128)(2,1)S(1)}, bf16[1,1,4,128,512]{4,3,2,1,0:T(8,128)(2,1)}, u32[]{:S(2)}) copy-start(bf16[1,1,4,128,512]{4,3,2,1,0:T(8,128)(2,1)} %param.6) | copy-start | bytes 1572868
  7.2 62.2 %all-gather.2.cloned.1.call-start = ((), (), s32[]{:S(2)}) async-start(), calls=%async_computation.6 | async-start | bytes 5898240 | tf_op jit(solution)/shard_map/all_gather | solution.py:102
  13.4 63.6 %all-to-all-start = ((bf16[1,8,64,512]{3,2,0,1:T(8,128)(2,1)}), bf16[1,8,64,512]{3,2,0,1:T(8,128)(2,1)S(1)}, u32[]{:S(2)}, u32[]{:S(2)}) async-start(bf16[1,8,64,512]{3,2,0,1:T(8,128)(2,1)} %fusion.15), calls=%async_computation | async-start | bytes 1048576 | tf_op jit(solution)/shard_map/all_to_all | solution.py:116
  19.8 140.7 %reduce-scatter.15.cloned.1.call-start = ((), (), s32[]{:S(2)}) async-start(), calls=%async_computation.10 | async-start | bytes 3538944
  35.9 37.4 %copy-start.12 = (bf16[1,4,128,512]{3,2,1,0:T(8,128)(2,1)S(1)}, bf16[1,4,128,512]{3,2,1,0:T(8,128)(2,1)}, u32[]{:S(2)}) copy-start(bf16[1,4,128,512]{3,2,1,0:T(8,128)(2,1)} %copy.42) | copy-start | bytes 1572868
  36.9 35.9 %copy-start.13 = (bf16[1,4,128,512]{3,2,1,0:T(8,128)(2,1)S(1)}, bf16[1,4,128,512]{3,2,1,0:T(8,128)(2,1)}, u32[]{:S(2)}) copy-start(bf16[1,4,128,512]{3,2,1,0:T(8,128)(2,1)} %copy.41) | copy-start | bytes 1572868
  69.4 3.4 %copy-start = (bf16[4608,512]{1,0:T(8,128)(2,1)S(1)}, bf16[4608,512]{1,0:T(8,128)(2,1)}, u32[]{:S(2)}) copy-start(bf16[4608,512]{1,0:T(8,128)(2,1)} %all-gather.2.cloned.1.call-done) | copy-start | bytes 14155780
  72.8 1.4 copy-start.11
  73.3 1.4 copy-start.10
  73.7 1.4 copy-start.9
  74.2 1.4 copy-start.8
  74.7 2.3 copy-start.14
  74.7 2.3 copy-start.15
  122.0 139.5 %reduce-scatter.13.cloned.1.call-start = ((), (), s32[]{:S(2)}) async-start(), calls=%async_computation.9 | async-start | bytes 10616832
  123.5 5.9 %copy-start.3 = (bf16[1,1,4,128,512]{4,3,2,1,0:T(8,128)(2,1)S(1)}, bf16[1,1,4,128,512]{4,3,2,1,0:T(8,128)(2,1)}, u32[]{:S(2)}) copy-start(bf16[1,1,4,128,512]{4,3,2,1,0:T(8,128)(2,1)} %param.6) | copy-start | bytes 1572868
  146.5 142.4 %reduce-scatter.11.cloned.1.call-start = ((), (), s32[]{:S(2)}) async-start(), calls=%async_computation.8 | async-start | bytes 983040 | tf_op jit(solution)/shard_map/reduce_scatter | solution.py:136
  162.7 166.6 %reduce-scatter.9.cloned.1.call-start = ((), (), s32[]{:S(2)}) async-start(), calls=%async_computation.7 | async-start | bytes 2949120 | tf_op jit(solution)/shard_map/reduce_scatter | solution.py:135
  261.5 8.3 %slice-start = ((s8[4718592]{0:T(1024)(128)(4,1)}), s8[524288]{0:T(1024)(128)(4,1)S(1)}, s32[]{:S(2)}) async-start(s8[4718592]{0:T(1024)(128)(4,1)} %bitcast.214), calls=%async_computation.11 | async-start | bytes 1048576
  264.5 5.3 %slice-start.1 = ((s8[4718592]{0:T(1024)(128)(4,1)}), s8[4194304]{0:T(1024)(128)(4,1)S(1)}, s32[]{:S(2)}) async-start(s8[4718592]{0:T(1024)(128)(4,1)} %bitcast.214), calls=%async_computation.12 | async-start | bytes 8388608
  266.3 4.0 %copy-start.7 = (bf16[1,4,128,512]{3,2,1,0:T(8,128)(2,1)S(1)}, bf16[1,4,128,512]{3,2,1,0:T(8,128)(2,1)}, u32[]{:S(2)}) copy-start(bf16[1,4,128,512]{3,2,1,0:T(8,128)(2,1)} %get-tuple-element.24) | copy-start | bytes 1572868
  268.0 2.8 copy-start.6
  269.8 1.5 copy-start.5
  270.3 1.5 copy-start.4
Sparse Core Ops, SparseCore 0:
  9.8 59.5 all-gather.1
  122.1 38.3 reduce-scatter.14
  162.8 98.6 reduce-scatter.12
  264.3 24.6 reduce-scatter.10
  291.8 37.3 reduce-scatter.8
where the time goes:
time: 339 us; the launch traced here: 338 us
  waiting for transfers between devices  196 us (58%)
  local copies, waits for them, and re-layouts  49.4 us (15%)
  matrix products  36.5 us (11%)
  blocking collectives  20 us (6%)
  other arithmetic  14.8 us (4%)
  between operations  14.3 us (4%)
  starting transfers between devices  6.55 us (2%)
    unnamed x7, waiting for transfers between devices  109 us
    reduce_scatter x1, waiting for transfers between devices, shards(): lax.psum_scatter(partial_pair[0], 'dp', scatter_dimension=0, tiled=True)  38.6 us
    all_gather x1, waiting for transfers between devices, shards(): weights = lax.all_gather(w_spatial, 'dp', axis=1, tiled=True)  32.4 us
    unnamed x47, local copies, waits for them, and re-layouts  27.9 us
    all_to_all x1, blocking collectives, shards(): tiles = lax.all_to_all(act, 'wide', split_axis=2, concat_axis=1, tiled=True)  20 us
    slice x9, local copies, waits for them, and re-layouts, spatial_forward(): padded[:, row_off:row_off + row_count, col_off:col_off + col_count, :]  16.8 us
    reduce_scatter x1, waiting for transfers between devices, shards(): lax.psum_scatter(partial_pair[1], 'dp', scatter_dimension=0, tiled=True)  15.9 us
    dot_general x9, matrix products, spatial_backward(): lax.dot_general(window, grad_flat, CONTRACT_ROWS, preferred_element_type=...  13.3 us
  transfers between devices with their start and end apart: 6, of which 5 were waited for; matrix products, arithmetic and copies ran while one was open for 22% of the time, Pallas kernels for 0%

commit v1 on v0

--- a/solution.py
+++ b/solution.py
@@ -107,7 +107,10 @@
         .astype(jnp.bfloat16)
         .reshape(group_count, frame_count, row_count * col_count, chan_count)
     )
-    tiles = lax.all_to_all(act, "wide", split_axis=2, concat_axis=1, tiled=True)
+    tiles = jnp.concatenate(
+        lax.all_to_all(jnp.stack(jnp.split(act, lax.axis_size("wide"), axis=2)), "wide", 0, 0),
+        axis=1,
+    )
     tile_shape = tiles.shape
     by_clip = tiles.reshape(-1, FRAMES, tile_shape[2], tile_shape[3])
     grad_clipwise = grad_out.reshape(by_clip.shape)

time: 339 us -> 324 us (0.956)
  local copies, waits for them, and re-layouts: 49.4 us -> 40.2 us
  other arithmetic: 14.8 us -> 9.23 us
    unnamed x47 -> x50, local copies, waits for them, and re-layouts: 27.9 us -> 20.4 us
    unnamed x2 -> x1, other arithmetic: 5.56 us -> 0.01 us
  transfers between devices with their start and end apart: 6 -> 6, of which waited for: 5 -> 5; matrix products, arithmetic and copies ran while one was open for 22% -> 23% of each run, Pallas kernels for 0% -> 0%
where the time goes in v1:
time: 324 us; the launch traced here: 323 us
  waiting for transfers between devices  196 us (60%)
  local copies, waits for them, and re-layouts  40.2 us (12%)
  matrix products  36.6 us (11%)
  blocking collectives  19.7 us (6%)
  between operations  14.3 us (4%)
  other arithmetic  9.23 us (3%)
  starting transfers between devices  6.73 us (2%)
    unnamed x7, waiting for transfers between devices  109 us
    reduce_scatter x1, waiting for transfers between devices, shards(): lax.psum_scatter(partial_pair[0], 'dp', scatter_dimension=0, tiled=True)  38.6 us
    all_gather x1, waiting for transfers between devices, shards(): weights = lax.all_gather(w_spatial, 'dp', axis=1, tiled=True)  32.4 us
    unnamed x50, local copies, waits for them, and re-layouts  20.4 us
    all_to_all x1, blocking collectives, shards(): lax.all_to_all(jnp.stack(jnp.split(act, lax.axis_size('wide'), axis=2)),...  19.7 us
    slice x9, local copies, waits for them, and re-layouts, spatial_forward(): padded[:, row_off:row_off + row_count, col_off:col_off + col_count, :]  16.9 us
    reduce_scatter x1, waiting for transfers between devices, shards(): lax.psum_scatter(partial_pair[1], 'dp', scatter_dimension=0, tiled=True)  15.9 us
    dot_general x9, matrix products, spatial_backward(): lax.dot_general(window, grad_flat, CONTRACT_ROWS, preferred_element_type=...  13.3 us
  transfers between devices with their start and end apart: 6, of which 5 were waited for; matrix products, arithmetic and copies ran while one was open for 23% of the time, Pallas kernels for 0%

profile of v1, /device:TPU:0, one launch (start us, length us, event | category | flops | bytes accessed | tf_op | source)
XLA Modules:
  0.0 322.8 jit_solution(10546165293153323364)
XLA Ops:
  11.1 2.3 fusion.15
  13.4 6.4 %all-to-all-start = ((bf16[1,8,64,512]{3,2,0,1:T(8,128)(2,1)}), bf16[1,8,64,512]{3,2,0,1:T(8,128)(2,1)S(1)}, u32[]{:S(2)}, u32[]{:S(2)}) async-start(bf16[1,8,64,512]{3,2,0,1:T(8,128)(2,1)} %fusion.15), calls=%async_computation | async-start | bytes 1048576 | tf_op jit(solution)/shard_map/all_to_all | solution.py:119
  20.1 2.5 pad_slice_fusion
  22.7 2.1 copy.32
  24.7 2.0 copy.26
  26.8 2.1 copy.27
  28.8 2.0 copy.28
  30.9 2.0 copy.29
  32.9 2.1 copy.30
  37.0 32.4 %all-gather.2.cloned.1.call-done = bf16[4608,512]{1,0:T(8,128)(2,1)} async-done(((bf16[4608,128]{1,0:T(8,128)(2,1)}), bf16[4608,512]{1,0:T(8,128)(2,1)}) %all-gather.2.cloned.1.call-update) | async-done | bytes 4718608 | tf_op jit(solution)/shard_map/all_gather | solution.py:102
  69.4 1.8 fusion.56
  80.2 19.7 %all_to_all.14 = bf16[8,1,1,64,512]{4,3,2,1,0:T(8,128)(2,1)S(1)} all-to-all(bf16[8,1,1,64,512]{4,3,2,1,0:T(8,128)(2,1)S(1)} %fusion.66), channel_id=1, replica_groups=mesh['dp'=4,'wide'=8] {'wide'}, dimensions={0} | all-to-all | bytes 1048576 | tf_op jit(solution)/shard_map/all_to_all | solution.py:111
  101.4 2.0 pad_maximum_fusion
  103.3 3.6 %copy.38 = f32[1536,512]{0,1:T(8,128)} copy(f32[1536,512]{1,0:T(8,128)} %pad_maximum_fusion) | data formatting | bytes 6291456
  122.0 9.7 %copy.36 = f32[4608,512]{0,1:T(8,128)} copy(f32[4608,512]{1,0:T(8,128)} %fusion) | data formatting | bytes 18874368
  131.7 13.7 %reduce-scatter.15.cloned.1.call-done = f32[64,1536]{1,0:T(8,128)} async-done(((f32[512,1536]{1,0:T(8,128)}), f32[64,1536]{1,0:T(8,128)}) %reduce-scatter.15.cloned.1.call-update) | async-done | bytes 393232
  145.4 2.2 copy.39
  148.4 1.9 pad_slice_fusion.8
  151.8 94.7 %reduce-scatter.13.cloned.1.call-done = f32[64,4608]{1,0:T(8,128)} async-done(((f32[512,4608]{1,0:T(8,128)}), f32[64,4608]{1,0:T(8,128)}) %reduce-scatter.13.cloned.1.call-update) | async-done | bytes 1179664
  246.6 2.9 copy.37
  249.5 1.8 convolution_add_fusion.7
  253.1 1.7 convolution_add_fusion.5
  258.1 15.9 %reduce-scatter.11.cloned.1.call-done = f32[384,64]{1,0:T(8,128)} async-done(((f32[1536,64]{1,0:T(8,128)}), f32[384,64]{1,0:T(8,128)}) %reduce-scatter.11.cloned.1.call-update) | async-done | bytes 98320 | tf_op jit(solution)/shard_map/reduce_scatter | solution.py:139
  275.7 38.6 %reduce-scatter.9.cloned.1.call-done = f32[1152,64]{1,0:T(8,128)} async-done(((f32[4608,64]{1,0:T(8,128)}), f32[1152,64]{1,0:T(8,128)}) %reduce-scatter.9.cloned.1.call-update) | async-done | bytes 294928 | tf_op jit(solution)/shard_map/reduce_scatter | solution.py:138
  (117 shorter events, 42.4 us)
Async XLA Ops:
  7.2 3.9 %copy-start.1 = (bf16[1,8,64,512]{3,2,1,0:T(8,128)(2,1)S(1)}, bf16[1,8,64,512]{3,2,1,0:T(8,128)(2,1)}, u32[]{:S(2)}) copy-start(bf16[1,8,64,512]{3,2,1,0:T(8,128)(2,1)} %param.11) | copy-start | bytes 1572868
  7.2 12.7 %copy-start.2 = (bf16[1,1,4,128,512]{4,3,2,1,0:T(8,128)(2,1)S(1)}, bf16[1,1,4,128,512]{4,3,2,1,0:T(8,128)(2,1)}, u32[]{:S(2)}) copy-start(bf16[1,1,4,128,512]{4,3,2,1,0:T(8,128)(2,1)} %param.6) | copy-start | bytes 1572868
  7.2 62.2 %all-gather.2.cloned.1.call-start = ((), (), s32[]{:S(2)}) async-start(), calls=%async_computation.6 | async-start | bytes 5898240 | tf_op jit(solution)/shard_map/all_gather | solution.py:102
  13.4 63.6 %all-to-all-start = ((bf16[1,8,64,512]{3,2,0,1:T(8,128)(2,1)}), bf16[1,8,64,512]{3,2,0,1:T(8,128)(2,1)S(1)}, u32[]{:S(2)}, u32[]{:S(2)}) async-start(bf16[1,8,64,512]{3,2,0,1:T(8,128)(2,1)} %fusion.15), calls=%async_computation | async-start | bytes 1048576 | tf_op jit(solution)/shard_map/all_to_all | solution.py:119
  19.8 125.7 %reduce-scatter.15.cloned.1.call-start = ((), (), s32[]{:S(2)}) async-start(), calls=%async_computation.10 | async-start | bytes 3538944
  36.0 37.3 %copy-start.12 = (bf16[1,4,128,512]{3,2,1,0:T(8,128)(2,1)S(1)}, bf16[1,4,128,512]{3,2,1,0:T(8,128)(2,1)}, u32[]{:S(2)}) copy-start(bf16[1,4,128,512]{3,2,1,0:T(8,128)(2,1)} %copy.28) | copy-start | bytes 1572868
  37.0 35.8 %copy-start.13 = (bf16[1,4,128,512]{3,2,1,0:T(8,128)(2,1)S(1)}, bf16[1,4,128,512]{3,2,1,0:T(8,128)(2,1)}, u32[]{:S(2)}) copy-start(bf16[1,4,128,512]{3,2,1,0:T(8,128)(2,1)} %copy.27) | copy-start | bytes 1572868
  69.4 3.4 %copy-start = (bf16[4608,512]{1,0:T(8,128)(2,1)S(1)}, bf16[4608,512]{1,0:T(8,128)(2,1)}, u32[]{:S(2)}) copy-start(bf16[4608,512]{1,0:T(8,128)(2,1)} %all-gather.2.cloned.1.call-done) | copy-start | bytes 14155780
  72.8 1.4 copy-start.11
  73.3 1.4 copy-start.10
  73.7 1.4 copy-start.9
  74.2 1.4 copy-start.8
  74.7 2.3 copy-start.14
  74.7 2.3 copy-start.15
  107.0 139.6 %reduce-scatter.13.cloned.1.call-start = ((), (), s32[]{:S(2)}) async-start(), calls=%async_computation.9 | async-start | bytes 10616832
  108.7 5.9 %copy-start.3 = (bf16[1,1,4,128,512]{4,3,2,1,0:T(8,128)(2,1)S(1)}, bf16[1,1,4,128,512]{4,3,2,1,0:T(8,128)(2,1)}, u32[]{:S(2)}) copy-start(bf16[1,1,4,128,512]{4,3,2,1,0:T(8,128)(2,1)} %param.6) | copy-start | bytes 1572868
  131.7 142.3 %reduce-scatter.11.cloned.1.call-start = ((), (), s32[]{:S(2)}) async-start(), calls=%async_computation.8 | async-start | bytes 983040 | tf_op jit(solution)/shard_map/reduce_scatter | solution.py:139
  147.6 166.6 %reduce-scatter.9.cloned.1.call-start = ((), (), s32[]{:S(2)}) async-start(), calls=%async_computation.7 | async-start | bytes 2949120 | tf_op jit(solution)/shard_map/reduce_scatter | solution.py:138
  246.5 8.3 %slice-start = ((s8[4718592]{0:T(1024)(128)(4,1)}), s8[524288]{0:T(1024)(128)(4,1)S(1)}, s32[]{:S(2)}) async-start(s8[4718592]{0:T(1024)(128)(4,1)} %bitcast.241), calls=%async_computation.11 | async-start | bytes 1048576
  249.5 5.3 %slice-start.1 = ((s8[4718592]{0:T(1024)(128)(4,1)}), s8[4194304]{0:T(1024)(128)(4,1)S(1)}, s32[]{:S(2)}) async-start(s8[4718592]{0:T(1024)(128)(4,1)} %bitcast.241), calls=%async_computation.12 | async-start | bytes 8388608
  251.3 4.0 %copy-start.7 = (bf16[1,4,128,512]{3,2,1,0:T(8,128)(2,1)S(1)}, bf16[1,4,128,512]{3,2,1,0:T(8,128)(2,1)}, u32[]{:S(2)}) copy-start(bf16[1,4,128,512]{3,2,1,0:T(8,128)(2,1)} %get-tuple-element.21) | copy-start | bytes 1572868
  253.1 2.8 copy-start.6
  254.8 1.5 copy-start.5
  255.3 1.5 copy-start.4
Sparse Core Ops, SparseCore 0:
  9.8 59.5 all-gather.1
  107.1 38.3 reduce-scatter.14
  147.7 98.7 reduce-scatter.12
  249.3 24.6 reduce-scatter.10
  276.9 37.3 reduce-scatter.8
